TPU v7x, 32 devices: a whole 2x2x4 slice. The times are simulated.
32 devices in a mesh: dp: 4 (over y, x), seq: 4 (over z), expert: 2 (over core).
Axes of the slice: x: 2, y: 2, z: 4, core: 2. Of those that a mesh axis runs over, the one named last changes fastest.
Arguments:
- queries: bfloat16 [8, 512, 2048], P(('dp', 'expert'), 'seq'), may hold values from -135 to 135
- keys: bfloat16 [8, 512, 2048], P(('dp', 'expert'), 'seq'), may hold values from -5 to 5
- values: bfloat16 [8, 512, 2048], P(('dp', 'expert'), 'seq'), may hold values from -6 to 6
- resid: bfloat16 [8, 512, 2048], P(('dp', 'expert'), 'seq'), may hold values from -20 to 20
- cotangent: bfloat16 [8, 512, 2048], P(('dp', 'expert'), 'seq'), may hold values from -0.3125 to 0.3125
- zone_ids: int32 [8, 512, 1], P(('dp', 'expert'), 'seq'), may hold values from 0 to 7; in each aligned block of 128 rows (0 to 127, 128 to 255, ..., all dimensions but the last counted through in order) at most 34 rows name the same one
- norm_gain: float32 [2048], replicated, may hold values from 0.1 to 1.9
- w_in: bfloat16 [8, 2048, 4096], P(('seq', 'expert'), None, 'dp'), may hold values from -0.125 to 0.125
- w_out: bfloat16 [8, 4096, 2048], P(('seq', 'expert'), 'dp'), may hold values from -0.09375 to 0.09375
Outputs:
- layer_out: bfloat16 [8, 512, 2048], P(('dp', 'expert'), 'seq')
- grad_w_in: bfloat16 [8, 2048, 4096], P(('seq', 'expert'), None, 'dp')
- grad_w_out: bfloat16 [8, 4096, 2048], P(('seq', 'expert'), 'dp')
Inputs may be any that keep to these rules, and one draw needn't show every extreme that they name: `zone_ids`: among the tokens of one device at most 34 name the same expert, and that count is reached.
All inputs are finite; a program needn't handle non-finite values.
Results may differ from a plain program's by a relative error of at most 0.0085.
Values may be sent and summed in bfloat16 or wider, within the bound.
A program may use at most 128 MiB of HBM per device.

v0:
```python
import math

import jax
import jax.numpy as jnp
from jax import lax
from jax.sharding import PartitionSpec as P

HEADS = 16


epsilon = 1e-05


def shards(queries, keys, values, resid, cotangent, zone_ids, norm_gain, w_in, w_out):
    local_rows = queries.shape[1]
    model_width = queries.shape[2]
    head_dim = model_width // HEADS
    score_scale = 1.0 / math.sqrt(head_dim)
    q_heads = queries[0].reshape(local_rows, HEADS, head_dim)
    peak_now = jnp.full((HEADS, local_rows), -jnp.inf, jnp.float32)
    totals = jnp.zeros((HEADS, local_rows), jnp.float32)
    accum = jnp.zeros((HEADS, local_rows, head_dim), jnp.float32)
    key_block = lax.all_gather(keys, "seq", axis=1, tiled=True)
    value_block = lax.all_gather(values, "seq", axis=1, tiled=True)
    count = key_block.shape[1]
    k_heads = key_block[0].reshape(count, HEADS, head_dim)
    v_heads = value_block[0].reshape(count, HEADS, head_dim)
    scores = (
        jnp.einsum("shd,thd->hst", q_heads, k_heads, preferred_element_type=jnp.float32)
        * score_scale
    )
    newest = jnp.max(scores, axis=-1)
    factor = jnp.exp(peak_now - newest)
    weights = jnp.exp(scores - newest[..., None])
    totals = totals * factor + jnp.sum(weights, axis=-1)
    accum = accum * factor[..., None] + jnp.einsum(
        "hst,thd->hsd", weights.astype(jnp.bfloat16), v_heads, preferred_element_type=jnp.float32
    )
    peak_now, totals, accum = (newest, totals, accum)
    attended = (accum / totals[..., None]).transpose(1, 0, 2).reshape(local_rows, model_width)
    mixed = resid[0].astype(jnp.float32) + attended
    mean_sq = jnp.mean(mixed * mixed, axis=-1, keepdims=True)
    normed = (mixed * lax.rsqrt(mean_sq + epsilon) * norm_gain).astype(jnp.bfloat16)
    owners = lax.axis_size("seq") * lax.axis_size("expert")
    groups = lax.axis_size("dp")
    capacity = 2 * local_rows // owners + 2
    zone_of = zone_ids[0, :, 0]
    expert_hot = (zone_of[:, None] == jnp.arange(owners, dtype=jnp.int32)[None, :]).astype(
        jnp.int32
    )
    ranking = jnp.cumsum(expert_hot, axis=0) - 1
    slot_index = jnp.sum(ranking * expert_hot, axis=1)
    target = zone_of * capacity + slot_index
    placing = (target[None, :] == jnp.arange(owners * capacity, dtype=jnp.int32)[:, None]).astype(
        jnp.bfloat16
    )
    send_x = jnp.dot(placing, normed, preferred_element_type=jnp.float32).astype(jnp.bfloat16)
    send_g = jnp.dot(placing, cotangent[0], preferred_element_type=jnp.float32).astype(jnp.bfloat16)
    send_x = send_x.reshape(owners, capacity, model_width)
    send_g = send_g.reshape(owners, capacity, model_width)
    row_x, row_g = (
        lax.all_to_all(send_x, ("seq", "expert"), split_axis=0, concat_axis=0, tiled=True),
        lax.all_to_all(send_g, ("seq", "expert"), split_axis=0, concat_axis=0, tiled=True),
    )
    arrived_x, arrived_g = (
        lax.all_gather(row_x, "dp", axis=0, tiled=True),
        lax.all_gather(row_g, "dp", axis=0, tiled=True),
    )
    slot_count = groups * owners * capacity
    inputs = arrived_x.reshape(slot_count, model_width)
    grads_in = arrived_g.reshape(slot_count, model_width)
    w_first = w_in[0]
    w_second = w_out[0]
    pre_act = jnp.dot(inputs, w_first, preferred_element_type=jnp.float32)
    activated, pull_back = jax.vjp(jax.nn.gelu, pre_act)
    hidden = activated.astype(jnp.bfloat16)
    back_proj = lax.dot_general(
        grads_in, w_second, (((1,), (1,)), ((), ())), preferred_element_type=jnp.float32
    )
    d_pre = pull_back(back_proj)[0].astype(jnp.bfloat16)
    grad_first = lax.dot_general(
        inputs, d_pre, (((0,), (0,)), ((), ())), preferred_element_type=jnp.float32
    ).astype(jnp.bfloat16)
    grad_second = lax.dot_general(
        hidden, grads_in, (((0,), (0,)), ((), ())), preferred_element_type=jnp.float32
    ).astype(jnp.bfloat16)
    summed = lax.psum_scatter(
        jnp.dot(hidden, w_second, preferred_element_type=jnp.float32).astype(jnp.bfloat16),
        "dp",
        scatter_dimension=0,
        tiled=True,
    )
    returned = lax.all_to_all(
        summed.reshape(owners, capacity, model_width),
        ("seq", "expert"),
        split_axis=0,
        concat_axis=0,
        tiled=True,
    )
    expert_rows = lax.dot_general(
        placing,
        returned.reshape(owners * capacity, model_width),
        (((0,), (0,)), ((), ())),
        preferred_element_type=jnp.float32,
    )
    layer_out = (mixed + expert_rows).astype(jnp.bfloat16)[None]
    return (layer_out, grad_first[None], grad_second[None])


def solution(mesh):
    placed = (
        P(("dp", "expert"), "seq", None),
        P(("dp", "expert"), "seq", None),
        P(("dp", "expert"), "seq", None),
        P(("dp", "expert"), "seq", None),
        P(("dp", "expert"), "seq", None),
        P(("dp", "expert"), "seq", None),
        P(),
        P(("seq", "expert"), None, "dp"),
        P(("seq", "expert"), "dp", None),
    )
    return jax.shard_map(
        shards,
        mesh=mesh,
        in_specs=placed,
        out_specs=(
            P(("dp", "expert"), "seq", None),
            P(("seq", "expert"), None, "dp"),
            P(("seq", "expert"), "dp", None),
        ),
        check_vma=False,
    )
```

profile of v0, /device:TPU:25, one launch (start us, length us, event | category | flops | bytes accessed | tf_op | source)
XLA Modules:
  0.0 367.2 jit_solution(17556214826301399096)
XLA Ops:
  7.2 0.0 all-gather.5.cloned.1.call-start
  7.2 2.1 copy.22
  9.3 0.0 all-gather.5.cloned.1.call-update
  9.3 0.0 all-gather.7.cloned.1.call-start
  9.4 0.7 all-gather.7.cloned.1.call-update
  10.1 0.0 all-gather.9.cloned.1.call-start
  10.1 1.1 copy.33
  11.3 2.2 copy.27
  13.5 0.1 fusion.42
  13.6 0.2 reduce_window_sum.11
  13.8 0.2 select_reduce_fusion
  14.0 40.7 %all-gather.5.cloned.1.call-done = bf16[1,512,2048]{1,2,0:T(8,128)(2,1)} async-done(((bf16[1,128,2048]{1,2,0:T(8,128)(2,1)}), bf16[1,512,2048]{1,2,0:T(8,128)(2,1)}) %all-gather.5.cloned.1.call-update) | async-done | bytes 2097168 | tf_op jit(solution)/shard_map/all_gather | solution.py:23
  54.7 2.4 multiply_reduce_fusion
  57.1 2.0 copy-done.2
  59.1 1.3 fusion.14
  60.4 40.7 %all-gather.7.cloned.1.call-done = bf16[1,512,2048]{2,1,0:T(8,128)(2,1)} async-done(((bf16[1,128,2048]{2,1,0:T(8,128)(2,1)}), bf16[1,512,2048]{2,1,0:T(8,128)(2,1)}) %all-gather.7.cloned.1.call-update) | async-done | bytes 2097168 | tf_op jit(solution)/shard_map/all_gather | solution.py:24
  101.1 2.9 copy.25
  104.0 4.7 %multiply_reduce_fusion.1 = (f32[128]{0:T(128)S(1)}, f32[128,16,128]{0,2,1:T(8,128)}) fusion(f32[128,16,128]{0,2,1:T(8,128)} %bitcast.59, f32[128,16]{0,1:T(8,128)S(1)} %bitcast_add_fusion.2, bf16[512,16,128]{0,2,1:T(8,128)(2,1)S(1)} %bitcast.56, f32[16,128,512]{2,1,0:T(8,128)} %copy-done.2, f32[16,128]{1,0:T(8,128)S(1)} %get-tuple-element.3, ...), kind=kOutput, calls=%fused_computation.34 | convolution fusion | flops 272891776 | bytes 8413696 | tf_op jit(solution)/shard_map/hst,thd->hsd/dot_general | solution.py:36
  108.7 1.6 copy.26
  110.3 1.5 convolution_convert_fusion.2
  111.8 1.4 reshape.62
  113.2 34.6 %all_to_all.15 = bf16[8,34,2048]{2,1,0:T(8,128)(2,1)S(1)} all-to-all(bf16[8,34,2048]{2,1,0:T(8,128)(2,1)S(1)} %reshape.62), channel_id=1, replica_groups=mesh['dp'=4,'seq'=4,'expert'=2] {'seq','expert'}, dimensions={0} | all-to-all | bytes 2228224 | tf_op jit(solution)/shard_map/all_to_all | solution.py:62
  147.8 1.6 copy.28
  149.4 0.0 all-gather.9.cloned.1.call-update
  149.4 0.0 all-gather.11.cloned.1.call-start
  149.5 1.4 convolution_convert_fusion.1
  150.9 1.4 reshape.66
  152.3 34.6 %all_to_all.16 = bf16[8,34,2048]{2,1,0:T(8,128)(2,1)S(1)} all-to-all(bf16[8,34,2048]{2,1,0:T(8,128)(2,1)S(1)} %reshape.66), channel_id=1, replica_groups=mesh['dp'=4,'seq'=4,'expert'=2] {'seq','expert'}, dimensions={0} | all-to-all | bytes 2228224 | tf_op jit(solution)/shard_map/all_to_all | solution.py:63
  186.9 1.6 copy.30
  188.5 0.0 reduce-scatter.2.cloned.1.call-start
  188.6 16.2 %all-gather.9.cloned.1.call-done = bf16[32,34,2048]{2,0,1:T(8,128)(2,1)} async-done(((bf16[8,34,2048]{2,0,1:T(8,128)(2,1)}), bf16[32,34,2048]{2,0,1:T(8,128)(2,1)}) %all-gather.9.cloned.1.call-update) | async-done | bytes 4456464 | tf_op jit(solution)/shard_map/all_gather | solution.py:66
  204.8 7.1 %copy.29 = bf16[32,34,2048]{2,1,0:T(8,128)(2,1)} copy(bf16[32,34,2048]{2,0,1:T(8,128)(2,1)} %all-gather.9.cloned.1.call-done) | data formatting | bytes 8912896 | tf_op jit(solution)/shard_map/all_gather | solution.py:66
  211.9 7.6 %reshape.63 = bf16[1088,2048]{1,0:T(8,128)(2,1)} reshape(bf16[32,34,2048]{2,1,0:T(8,128)(2,1)} %copy.29) | data formatting | bytes 8912896 | tf_op jit(solution)/shard_map/reshape | solution.py:70
  219.4 8.0 %fusion.12 = f32[1088,1024]{1,0:T(8,128)S(1)} fusion(bf16[1088,2048]{1,0:T(8,128)(2,1)} %reshape.63, bf16[1,2048,1024]{2,1,0:T(8,128)(2,1)} %param.16), kind=kOutput, calls=%fused_computation.14 | convolution fusion | flops 4563402752 | bytes 13107200 | tf_op jit(solution)/shard_map/dot_general | solution.py:74
  227.4 2.1 copy-done.7
  229.5 6.7 %convolution_convert_fusion = bf16[1088,2048]{1,0:T(8,128)(2,1)} fusion(bf16[1,1024,2048]{2,1,0:T(8,128)(2,1)S(1)} %copy-done.6, f32[1088,1024]{1,0:T(8,128)S(1)} %fusion.12), kind=kOutput, calls=%fused_computation | convolution fusion | flops 4575657984 | bytes 13107200 | tf_op jit(solution)/shard_map/dot_general | solution.py:88
  236.3 0.0 reduce-scatter.2.cloned.1.call-update
  236.3 25.5 %all-gather.11.cloned.1.call-done = bf16[32,34,2048]{2,0,1:T(8,128)(2,1)} async-done(((bf16[8,34,2048]{2,0,1:T(8,128)(2,1)}), bf16[32,34,2048]{2,0,1:T(8,128)(2,1)}) %all-gather.11.cloned.1.call-update) | async-done | bytes 4456464 | tf_op jit(solution)/shard_map/all_gather | solution.py:67
  261.9 7.1 %copy.31 = bf16[32,34,2048]{2,1,0:T(8,128)(2,1)} copy(bf16[32,34,2048]{2,0,1:T(8,128)(2,1)} %all-gather.11.cloned.1.call-done) | data formatting | bytes 8912896 | tf_op jit(solution)/shard_map/all_gather | solution.py:67
  268.9 7.6 %reshape.67 = bf16[1088,2048]{1,0:T(8,128)(2,1)} reshape(bf16[32,34,2048]{2,1,0:T(8,128)(2,1)} %copy.31) | data formatting | bytes 8912896 | tf_op jit(solution)/shard_map/reshape | solution.py:71
  276.5 10.7 %convert_bitcast_fusion = bf16[1,1024,2048]{2,1,0:T(8,128)(2,1)} fusion(bf16[1088,2048]{1,0:T(8,128)(2,1)} %reshape.67, f32[1088,1024]{1,0:T(8,128)} %copy-done.7), kind=kOutput, calls=%fused_computation.16 | convolution fusion | flops 4575526912 | bytes 13107200 | tf_op jit(solution)/shard_map/dot_general | solution.py:84
  287.2 32.3 %reduce-scatter.2.cloned.1.call-done = bf16[272,2048]{1,0:T(8,128)(2,1)} async-done(((bf16[1088,2048]{1,0:T(8,128)(2,1)}), bf16[272,2048]{1,0:T(8,128)(2,1)}) %reduce-scatter.2.cloned.1.call-update) | async-done | bytes 1114128 | tf_op jit(solution)/shard_map/reduce_scatter | solution.py:87
  319.6 2.3 reshape.64
  321.9 5.5 %all-to-all-start.1 = ((bf16[8,34,2048]{2,1,0:T(8,128)(2,1)}), bf16[8,34,2048]{2,1,0:T(8,128)(2,1)S(1)}, u32[]{:S(2)}, u32[]{:S(2)}) async-start(bf16[8,34,2048]{2,1,0:T(8,128)(2,1)} %reshape.64), calls=%async_computation.2 | async-start | bytes 2621440 | tf_op jit(solution)/shard_map/all_to_all | solution.py:93
  327.4 18.7 %convert_bitcast_fusion.1 = bf16[1,2048,1024]{2,1,0:T(8,128)(2,1)} fusion(bf16[1088,2048]{1,0:T(8,128)(2,1)} %reshape.63, f32[1088,1024]{1,0:T(8,128)} %copy-done.7, bf16[1088,2048]{1,0:T(8,128)(2,1)} %reshape.67, bf16[1,1024,2048]{2,1,0:T(8,128)(2,1)} %param.17), kind=kOutput, calls=%fused_computation.17 | convolution fusion | flops 9151184896 | bytes 21757952 | tf_op jit(solution)/shard_map/dot_general | solution.py:81
  346.1 10.9 %all-to-all-done.1 = bf16[8,34,2048]{2,1,0:T(8,128)(2,1)S(1)} async-done(((bf16[8,34,2048]{2,1,0:T(8,128)(2,1)}), bf16[8,34,2048]{2,1,0:T(8,128)(2,1)S(1)}, u32[]{:S(2)}, u32[]{:S(2)}) %all-to-all-start.1) | async-done | bytes 1114144 | tf_op jit(solution)/shard_map/all_to_all | solution.py:93
  357.0 1.2 reshape.65
  358.2 2.5 fusion.17
  (19 shorter events, 0.1 us)
Async XLA Ops:
  7.2 142.3 %copy-start = (bf16[1,128,2048]{2,1,0:T(8,128)(2,1)S(1)}, bf16[1,128,2048]{2,1,0:T(8,128)(2,1)}, u32[]{:S(2)}) copy-start(bf16[1,128,2048]{2,1,0:T(8,128)(2,1)} %param.13) | copy-start | bytes 1572868
  7.2 6.3 %copy-start.5 = (s32[1,128,1]{1,2,0:T(1,128)S(1)}, s32[1,128,1]{1,2,0:T(1,128)}, u32[]{:S(2)}) copy-start(s32[1,128,1]{1,2,0:T(1,128)} %param.14) | copy-start | bytes 1540
  7.2 47.5 %all-gather.5.cloned.1.call-start = ((), (), s32[]{:S(2)}) async-start(), calls=%async_computation.4 | async-start | bytes 2621440 | tf_op jit(solution)/shard_map/all_gather | solution.py:23
  9.3 91.7 %all-gather.7.cloned.1.call-start = ((), (), s32[]{:S(2)}) async-start(), calls=%async_computation.5 | async-start | bytes 2621440 | tf_op jit(solution)/shard_map/all_gather | solution.py:24
  10.1 194.7 %all-gather.9.cloned.1.call-start = ((), (), s32[]{:S(2)}) async-start(), calls=%async_computation.6 | async-start | bytes 5570560 | tf_op jit(solution)/shard_map/all_gather | solution.py:66
  57.0 2.0 copy-start.2
  103.9 6.3 %copy-start.3 = (bf16[1,128,2048]{2,1,0:T(8,128)(2,1)S(1)}, bf16[1,128,2048]{2,1,0:T(8,128)(2,1)}, u32[]{:S(2)}) copy-start(bf16[1,128,2048]{2,1,0:T(8,128)(2,1)} %param.12) | copy-start | bytes 1572868
  103.9 6.3 %copy-start.4 = (f32[2048]{0:T(1024)S(1)}, f32[2048]{0:T(1024)}, u32[]{:S(2)}) copy-start(f32[2048]{0:T(1024)} %param.15) | copy-start | bytes 24580
  149.4 112.4 %all-gather.11.cloned.1.call-start = ((), (), s32[]{:S(2)}) async-start(), calls=%async_computation.8 | async-start | bytes 5570560 | tf_op jit(solution)/shard_map/all_gather | solution.py:67
  188.5 131.0 %reduce-scatter.2.cloned.1.call-start = ((), (), s32[]{:S(2)}) async-start(), calls=%async_computation.7 | async-start | bytes 5570560 | tf_op jit(solution)/shard_map/reduce_scatter | solution.py:87
  219.4 10.1 %copy-start.6 = (bf16[1,1024,2048]{2,1,0:T(8,128)(2,1)S(1)}, bf16[1,1024,2048]{2,1,0:T(8,128)(2,1)}, u32[]{:S(2)}) copy-start(bf16[1,1024,2048]{2,1,0:T(8,128)(2,1)} %param.17) | copy-start | bytes 12582916
  227.4 2.1 copy-start.7
  321.9 35.1 %all-to-all-start.1 = ((bf16[8,34,2048]{2,1,0:T(8,128)(2,1)}), bf16[8,34,2048]{2,1,0:T(8,128)(2,1)S(1)}, u32[]{:S(2)}, u32[]{:S(2)}) async-start(bf16[8,34,2048]{2,1,0:T(8,128)(2,1)} %reshape.64), calls=%async_computation.2 | async-start | bytes 2621440 | tf_op jit(solution)/shard_map/all_to_all | solution.py:93
  327.4 33.3 %copy-start.1 = (bf16[1,128,2048]{2,1,0:T(8,128)(2,1)S(1)}, bf16[1,128,2048]{2,1,0:T(8,128)(2,1)}, u32[]{:S(2)}) copy-start(bf16[1,128,2048]{2,1,0:T(8,128)(2,1)} %param.13) | copy-start | bytes 1572868
Sparse Core Ops, SparseCore 0:
  10.1 44.4 all-gather.4
  56.2 44.7 all-gather.6
  149.5 55.2 all-gather.8
  207.1 54.7 all-gather.10
  264.8 54.7 reduce-scatter.1
where the time goes:
time: 372 us; the launch traced here: 367 us
  waiting for transfers between devices  167 us (45%)
  blocking collectives  69.2 us (19%)
  matrix products  56.7 us (15%)
  local copies, waits for them, and re-layouts  52.7 us (14%)
  between operations  13.9 us (4%)
  starting transfers between devices  5.75 us (2%)
    all_gather x1, waiting for transfers between devices, shards(): key_block = lax.all_gather(keys, 'seq', axis=1, tiled=True)  40.7 us
    all_gather x1, waiting for transfers between devices, shards(): value_block = lax.all_gather(values, 'seq', axis=1, tiled=True)  40.7 us
    all_to_all x1, blocking collectives, shards(): lax.all_to_all(send_x, ('seq', 'expert'), split_axis=0, concat_axis=0, ti...  34.6 us
    all_to_all x1, blocking collectives, shards(): lax.all_to_all(send_g, ('seq', 'expert'), split_axis=0, concat_axis=0, ti...  34.6 us
    reduce_scatter x1, waiting for transfers between devices, shards(): lax.psum_scatter(jnp.dot(hidden, w_second, preferred_element_type=jnp.flo...  32.3 us
    all_gather x1, waiting for transfers between devices, shards(): lax.all_gather(row_g, 'dp', axis=0, tiled=True)  25.5 us
    dot_general x1, matrix products, shards(): lax.dot_general(inputs, d_pre, (((0,), (0,)), ((), ())), preferred_elemen...  18.7 us
    all_gather x1, waiting for transfers between devices, shards(): lax.all_gather(row_x, 'dp', axis=0, tiled=True)  16.2 us
  transfers between devices with their start and end apart: 6, of which 6 were waited for; matrix products, arithmetic and copies ran while one was open for 23% of the time, Pallas kernels for 0%

commit v1 on v0

v1 whole, which is shorter than its diff:
```python
import functools
import math

import jax
import jax.numpy as jnp
from jax import lax
from jax.experimental import pallas as pl
from jax.experimental.pallas import tpu as pltpu
from jax.sharding import PartitionSpec as P

HEADS = 16
MESH = pl.DeviceIdType.MESH


epsilon = 1e-05


def remote(src, dst, send_sem, recv_sem, device):
    return pltpu.make_async_remote_copy(
        src_ref=src,
        dst_ref=dst,
        send_sem=send_sem,
        recv_sem=recv_sem,
        device_id=device,
        device_id_type=MESH,
    )


class Place:
    def __init__(self, sizes):
        self.groups, self.ring, self.pair = sizes
        self.owners = self.ring * self.pair
        self.dp = lax.axis_index("dp")
        self.seq = lax.axis_index("seq")
        self.me = self.seq * self.pair + lax.axis_index("expert")
        self.sides = (self.dp + 1 - 2 * (self.dp % 2), (self.dp + 2) % 4)

    def owner(self, index):
        return {"seq": index // self.pair, "expert": index % self.pair}

    def after(self, k):
        return (self.me + k) % self.owners

    def before(self, k):
        return (self.me + self.owners - k) % self.owners

    def greet(self):
        barrier = pltpu.get_barrier_semaphore()
        for k in range(1, self.owners):
            pl.semaphore_signal(
                barrier, inc=1, device_id=self.owner(self.after(k)), device_id_type=MESH
            )
        for side in self.sides:
            pl.semaphore_signal(barrier, inc=1, device_id={"dp": side}, device_id_type=MESH)
        pl.semaphore_wait(barrier, self.owners + 1)


class Dispatch:
    def __init__(self, place, send, out, sems):
        self.place, self.send, self.out = place, send, out
        self.z_send, self.z_recv, self.f_send, self.f_recv, self.r_send, self.r_recv, self.own = sems

    def slot(self, group, source):
        return self.out.at[group * self.place.owners + source]

    def along(self, k):
        p = self.place
        return remote(
            self.send.at[p.after(k)],
            self.slot(p.dp, p.me),
            self.z_send.at[k],
            self.z_recv.at[k],
            p.owner(p.after(k)),
        )

    def local(self):
        p = self.place
        return pltpu.make_async_copy(self.send.at[p.me], self.slot(p.dp, p.me), self.own)

    def forward(self, k, side):
        p = self.place
        src = self.send.at[p.me] if k == 0 else self.slot(p.dp, p.before(k))
        return remote(
            src,
            self.slot(p.dp, p.before(k)),
            self.f_send.at[k, side],
            self.f_recv.at[k, side],
            {"dp": p.sides[side]},
        )

    def relay(self, k):
        p = self.place
        come, go = k % 2, 1 - k % 2
        ref = self.slot(p.sides[come], p.before(k))
        return remote(ref, ref, self.r_send.at[k], self.r_recv.at[k], {"dp": p.sides[go]})

    def start(self):
        for k in range(1, self.place.owners):
            self.along(k).start()
        self.local().start()
        for side in range(2):
            self.forward(0, side).start()

    def pass_on(self, k):
        if k > 0:
            self.along(k).wait_recv()
            for side in range(2):
                self.forward(k, side).start()

    def pass_diagonal(self, k):
        self.forward(k, k % 2).wait_recv()
        self.relay(k).start()

    def finish(self):
        for k in range(self.place.owners):
            if k > 0:
                self.along(k).wait_send()
            self.forward(k, 0).wait_send()
            self.forward(k, 1).wait_send()
            self.forward(k, 1 - k % 2).wait_recv()
            self.relay(k).wait()
        self.local().wait()


def dispatch_sems(owners):
    dma = pltpu.SemaphoreType.DMA
    return [
        dma((owners,)),
        dma((owners,)),
        dma((owners, 2)),
        dma((owners, 2)),
        dma((owners,)),
        dma((owners,)),
        dma,
    ]


def attend_kernel(sizes, q, k, v, resid, gain, send_g, mixed, normed, arrived_g,
                  held, out, back, in_send, in_recv, own_sem, o_send, o_recv, *sems):
    place = Place(sizes)
    ring = place.ring
    heads, rows, width = held.shape[1], held.shape[3], held.shape[4]
    scale = 1.0 / math.sqrt(width)
    seq = place.seq

    def peer(j):
        return (seq + j) % ring

    def piece(kind, h, j):
        column = pl.multiple_of((peer(j) * heads + h) * width, width)
        return remote(
            (q, k, v)[kind].at[:, pl.ds(column, width)],
            held.at[kind, h, seq],
            in_send.at[kind, h, j - 1],
            in_recv.at[kind, h, j - 1],
            {"seq": peer(j)},
        )

    def own_piece(kind, h):
        column = pl.multiple_of((seq * heads + h) * width, width)
        return pltpu.make_async_copy(
            (q, k, v)[kind].at[:, pl.ds(column, width)], held.at[kind, h, seq], own_sem.at[kind, h]
        )

    def give_back(h, j):
        return remote(
            out.at[h, peer(j)],
            back.at[seq, h],
            o_send.at[h, j - 1],
            o_recv.at[h, j - 1],
            {"seq": peer(j)},
        )

    place.greet()
    tokens = Dispatch(place, send_g, arrived_g, sems)
    tokens.start()
    for h in range(heads):
        for kind in range(3):
            own_piece(kind, h).start()
            for j in range(1, ring):
                piece(kind, h, j).start()
    for n in range(place.owners):
        tokens.pass_on(n)
    relays = list(range(place.owners))
    for h in range(heads):
        for kind in range(3):
            own_piece(kind, h).wait()
            for j in range(1, ring):
                piece(kind, h, j).wait_recv()
        keys = held[1, h].reshape(ring * rows, width)
        vals = held[2, h].reshape(ring * rows, width)
        for j in range(ring):
            scores = (
                lax.dot_general(
                    held[0, h, j], keys, (((1,), (1,)), ((), ())), preferred_element_type=jnp.float32
                )
                * scale
            )
            weights = jnp.exp(scores - jnp.max(scores, axis=-1, keepdims=True))
            totals = jnp.sum(weights, axis=-1, keepdims=True)
            gained = jnp.dot(
                weights.astype(jnp.bfloat16), vals, preferred_element_type=jnp.float32
            )
            out[h, j] = (gained / totals).astype(jnp.bfloat16)
        for j in range(1, ring):
            give_back(h, j).start()
        back[seq, h] = out[h, seq]
        share = -(-place.owners // heads)
        for n in relays[h * share : (h + 1) * share]:
            tokens.pass_diagonal(n)
    for h in range(heads):
        for j in range(1, ring):
            give_back(h, j).wait_recv()
    step = 16

    @pl.loop(0, rows // step)
    def _(i):
        at = pl.ds(pl.multiple_of(i * step, step), step)
        total = jnp.zeros((step, 1), jnp.float32)
        for s in range(ring):
            for h in range(heads):
                cols = slice((s * heads + h) * width, (s * heads + h + 1) * width)
                value = resid[at, cols].astype(jnp.float32) + back[s, h, at, :].astype(jnp.float32)
                mixed[at, cols] = value
                total = total + jnp.sum(value * value, axis=-1, keepdims=True)
        factor = lax.rsqrt(total / resid.shape[1] + epsilon)
        normed[at, :] = (mixed[at, :] * factor * gain[...]).astype(jnp.bfloat16)

    for h in range(heads):
        for j in range(1, ring):
            give_back(h, j).wait_send()
            for kind in range(3):
                piece(kind, h, j).wait_send()
    tokens.finish()


def dispatch_kernel(sizes, send, arrived, *sems):
    place = Place(sizes)
    place.greet()
    tokens = Dispatch(place, send, arrived, sems)
    tokens.start()
    for n in range(place.owners):
        tokens.pass_on(n)
        if n > 0:
            tokens.pass_diagonal(n - 1)
    tokens.pass_diagonal(place.owners - 1)
    tokens.finish()


def combine_kernel(sizes, part, returned, first, mine, onward, second, a_send, a_recv, b_send,
                   b_recv, z_send, z_recv, own_sem):
    place = Place(sizes)
    owners = place.owners
    place.greet()

    def sides(k):
        return place.sides[k % 2], place.sides[1 - k % 2]

    def block(group, k):
        return part.at[group * owners + place.after(k)]

    def exchange(k, which):
        near, far = sides(k)
        other = (place.dp + 2) % 4 + 1 - 2 * (place.dp % 2)
        return remote(
            block(near if which == 0 else other, k),
            first.at[k, which],
            a_send.at[k, which],
            a_recv.at[k, which],
            {"dp": near},
        )

    def push(k):
        return remote(
            onward.at[k], second.at[k], b_send.at[k], b_recv.at[k], {"dp": sides(k)[1]}
        )

    def deliver(k):
        return remote(
            mine.at[k],
            returned.at[place.me],
            z_send.at[k],
            z_recv.at[k],
            place.owner(place.after(k)),
        )

    order = list(range(1, owners)) + [0]
    for k in order:
        exchange(k, 1).start()
        exchange(k, 0).start()

    def add(k):
        exchange(k, 1).wait_recv()
        far = sides(k)[1]
        onward[k] = (
            block(far, k)[...].astype(jnp.float32) + first[k, 1].astype(jnp.float32)
        ).astype(jnp.bfloat16)
        push(k).start()

    def close(k):
        exchange(k, 0).wait_recv()
        push(k).wait_recv()
        total = (
            block(place.dp, k)[...].astype(jnp.float32)
            + first[k, 0].astype(jnp.float32)
            + second[k].astype(jnp.float32)
        ).astype(jnp.bfloat16)
        mine[k] = total
        if k > 0:
            deliver(k).start()
        else:
            pltpu.make_async_copy(mine.at[0], returned.at[place.me], own_sem).start()

    lag = 2
    for n, k in enumerate(order):
        add(k)
        if n >= lag:
            close(order[n - lag])
    for k in order[owners - lag :]:
        close(k)
    for k in order:
        exchange(k, 0).wait_send()
        exchange(k, 1).wait_send()
        push(k).wait_send()
        if k > 0:
            deliver(k).wait()
    pltpu.make_async_copy(mine.at[0], returned.at[place.me], own_sem).wait()


def params(number):
    return pltpu.CompilerParams(
        collective_id=number, has_side_effects=True, vmem_limit_bytes=48 * 1024 * 1024
    )


ANY = pl.BlockSpec(memory_space=pl.ANY)
VMEM = pl.BlockSpec(memory_space=pltpu.VMEM)


def shards(sizes, queries, keys, values, resid, cotangent, zone_ids, norm_gain, w_in, w_out):
    rows = queries.shape[1]
    width = queries.shape[2]
    head_dim = width // HEADS
    groups, ring, pair = sizes
    owners = ring * pair
    heads = HEADS // ring
    capacity = 2 * rows // owners + 2
    padded = -(-capacity // 8) * 8
    dma = pltpu.SemaphoreType.DMA
    bf16, f32 = jnp.bfloat16, jnp.float32

    zone_of = zone_ids[0, :, 0]
    expert_hot = (zone_of[:, None] == jnp.arange(owners, dtype=jnp.int32)[None, :]).astype(
        jnp.int32
    )
    ranking = jnp.cumsum(expert_hot, axis=0) - 1
    slot_index = jnp.sum(ranking * expert_hot, axis=1)
    target = zone_of * padded + slot_index
    placing = (target[None, :] == jnp.arange(owners * padded, dtype=jnp.int32)[:, None]).astype(
        bf16
    )

    def placed(x):
        sent = jnp.dot(placing, x, preferred_element_type=f32).astype(bf16)
        return sent.reshape(owners, padded, width)

    slots = jax.ShapeDtypeStruct((groups * owners, padded, width), bf16)
    mixed, normed, arrived_g = pl.pallas_call(
        functools.partial(attend_kernel, sizes),
        out_shape=(
            jax.ShapeDtypeStruct((rows, width), f32),
            jax.ShapeDtypeStruct((rows, width), bf16),
            slots,
        ),
        in_specs=[ANY, ANY, ANY, VMEM, VMEM, VMEM],
        out_specs=(VMEM, VMEM, ANY),
        scratch_shapes=[
            pltpu.VMEM((3, heads, ring, rows, head_dim), bf16),
            pltpu.VMEM((heads, ring, rows, head_dim), bf16),
            pltpu.VMEM((ring, heads, rows, head_dim), bf16),
            dma((3, heads, ring - 1)),
            dma((3, heads, ring - 1)),
            dma((3, heads)),
            dma((heads, ring - 1)),
            dma((heads, ring - 1)),
            *dispatch_sems(owners),
        ],
        compiler_params=params(0),
        name="attend",
    )(queries[0], keys[0], values[0], resid[0], norm_gain[None, :], placed(cotangent[0]))

    arrived_x = pl.pallas_call(
        functools.partial(dispatch_kernel, sizes),
        out_shape=slots,
        in_specs=[VMEM],
        out_specs=ANY,
        scratch_shapes=dispatch_sems(owners),
        compiler_params=params(1),
        name="dispatch",
    )(placed(normed))

    slot_count = groups * owners * padded
    inputs = arrived_x.reshape(slot_count, width)
    grads_in = arrived_g.reshape(slot_count, width)
    w_first = w_in[0]
    w_second = w_out[0]
    pre_act = jnp.dot(inputs, w_first, preferred_element_type=f32)
    activated, pull_back = jax.vjp(jax.nn.gelu, pre_act)
    hidden = activated.astype(bf16)
    back_proj = lax.dot_general(
        grads_in, w_second, (((1,), (1,)), ((), ())), preferred_element_type=f32
    )
    d_pre = pull_back(back_proj)[0].astype(bf16)
    grad_first = lax.dot_general(
        inputs, d_pre, (((0,), (0,)), ((), ())), preferred_element_type=f32
    ).astype(bf16)
    grad_second = lax.dot_general(
        hidden, grads_in, (((0,), (0,)), ((), ())), preferred_element_type=f32
    ).astype(bf16)
    part = jnp.dot(hidden, w_second, preferred_element_type=f32).astype(bf16)

    returned = pl.pallas_call(
        functools.partial(combine_kernel, sizes),
        out_shape=jax.ShapeDtypeStruct((owners, padded, width), bf16),
        in_specs=[VMEM],
        out_specs=VMEM,
        scratch_shapes=[
            pltpu.VMEM((owners, 2, padded, width), bf16),
            pltpu.VMEM((owners, padded, width), bf16),
            pltpu.VMEM((owners, padded, width), bf16),
            pltpu.VMEM((owners, padded, width), bf16),
            dma((owners, 2)),
            dma((owners, 2)),
            dma((owners,)),
            dma((owners,)),
            dma((owners,)),
            dma((owners,)),
            dma,
        ],
        compiler_params=params(2),
        name="combine",
    )(part.reshape(groups * owners, padded, width))

    expert_rows = lax.dot_general(
        placing,
        returned.reshape(owners * padded, width),
        (((0,), (0,)), ((), ())),
        preferred_element_type=f32,
    )
    layer_out = (mixed + expert_rows).astype(bf16)[None]
    return (layer_out, grad_first[None], grad_second[None])


def solution(mesh):
    sizes = tuple(mesh.shape[name] for name in ("dp", "seq", "expert"))
    placed = (
        P(("dp", "expert"), "seq", None),
        P(("dp", "expert"), "seq", None),
        P(("dp", "expert"), "seq", None),
        P(("dp", "expert"), "seq", None),
        P(("dp", "expert"), "seq", None),
        P(("dp", "expert"), "seq", None),
        P(),
        P(("seq", "expert"), None, "dp"),
        P(("seq", "expert"), "dp", None),
    )
    return jax.shard_map(
        functools.partial(shards, sizes),
        mesh=mesh,
        in_specs=placed,
        out_specs=(
            P(("dp", "expert"), "seq", None),
            P(("seq", "expert"), None, "dp"),
            P(("seq", "expert"), "dp", None),
        ),
        check_vma=False,
    )
```

time: 372 us -> 266 us (0.72); the launches traced: 367 us -> 265 us
  Pallas kernels: 0 us -> 207 us
  waiting for transfers between devices: 167 us -> 0 us
  blocking collectives: 69.2 us -> 0 us
  local copies, waits for them, and re-layouts: 52.7 us -> 4.88 us
  between operations: 13.9 us -> 0.72 us
  matrix products: 56.7 us -> 50.6 us
  starting transfers between devices: 5.75 us -> 0 us
    pallas_call x0 -> x3, Pallas kernels: none -> 207 us  [the longest x1 79.2 us: shards(): pl.pallas_call(functools.partial(attend_kernel, sizes), out_shape=(jax.Sh...]
    all_gather x4 -> x0, waiting for transfers between devices: 123 us -> none  [the longest x1 40.7 us: shards(): key_block = lax.all_gather(keys, 'seq', axis=1, tiled=True)]
    all_to_all x2 -> x0, blocking collectives: 69.2 us -> none  [the longest x1 34.6 us: shards(): lax.all_to_all(send_x, ('seq', 'expert'), split_axis=0, concat_axis=0, ti...]
    reduce_scatter x1 -> x0, waiting for transfers between devices: 32.3 us -> none  [shards(): lax.psum_scatter(jnp.dot(hidden, w_second, preferred_element_type=jnp.flo...]
    reshape x7 -> x0, local copies, waits for them, and re-layouts: 22.9 us -> none  [the longest x1 7.56 us: shards(): grads_in = arrived_g.reshape(slot_count, model_width)]
    all_gather x3 -> x0, local copies, waits for them, and re-layouts: 17 us -> none  [the longest x1 7.07 us: shards(): lax.all_gather(row_x, 'dp', axis=0, tiled=True)]
    all_to_all x1 -> x0, waiting for transfers between devices: 10.9 us -> none  [shards(): lax.all_to_all(summed.reshape(owners, capacity, model_width), ('seq', 'ex...]
    dot_general x7 -> x5, matrix products: 27.3 us -> 19.2 us  [the longest x1 9.17 us: shards(): pre_act = jnp.dot(inputs, w_first, preferred_element_type=f32)]
  transfers between devices with their start and end apart: 6 -> 0, of which waited for: 6 -> 0; matrix products, arithmetic and copies ran while one was open for 23% -> 0% of each run, Pallas kernels for 0% -> 0%
where the time goes in v1:
time: 266 us; the launch traced here: 265 us
  Pallas kernels  207 us (78%)
  matrix products  50.6 us (19%)
  local copies, waits for them, and re-layouts  4.88 us (2%)
    pallas_call x1, Pallas kernels, shards(): pl.pallas_call(functools.partial(attend_kernel, sizes), out_shape=(jax.Sh...  79.2 us
    pallas_call x1, Pallas kernels, shards(): pl.pallas_call(functools.partial(combine_kernel, sizes), out_shape=jax.Sh...  69.8 us
    pallas_call x1, Pallas kernels, shards(): pl.pallas_call(functools.partial(dispatch_kernel, sizes), out_shape=slots...  57.5 us
    dot_general x1, matrix products, shards(): lax.dot_general(inputs, d_pre, (((0,), (0,)), ((), ())), preferred_elemen...  20 us
    dot_general x1, matrix products, shards(): lax.dot_general(hidden, grads_in, (((0,), (0,)), ((), ())), preferred_ele...  11.3 us
    dot_general x1, matrix products, shards(): pre_act = jnp.dot(inputs, w_first, preferred_element_type=f32)  9.17 us
    dot_general x1, matrix products, shards(): part = jnp.dot(hidden, w_second, preferred_element_type=f32).astype(bf16)  7.77 us

profile of v1, /device:TPU:25, one launch (start us, length us, event | category | flops | bytes accessed | tf_op | source)
XLA Modules:
  0.0 265.2 jit_solution(14081214810438640065)
XLA Ops:
  0.6 0.0 copy-start
  0.6 0.8 fusion.22
  1.4 0.2 reduce_window_sum.11
  1.6 0.8 select_reduce_fusion
  2.4 0.7 multiply_add_fusion
  3.1 0.0 copy-done
  3.1 0.5 convolution_convert_fusion.2
  3.6 0.0 copy-start.1
  3.6 1.0 copy-done.1
  4.7 0.0 copy-start.2
  4.7 1.0 copy-done.2
  5.7 0.0 copy-start.3
  5.7 1.0 copy-done.3
  6.7 0.0 copy-start.4
  6.7 1.0 copy-done.4
  7.8 0.0 copy-start.5
  7.8 0.7 copy-done.5
  8.5 0.0 copy-start.6
  8.5 79.2 %attend.1 = (f32[128,2048]{1,0:T(8,128)S(1)}, bf16[128,2048]{1,0:T(8,128)(2,1)S(1)}, bf16[32,40,2048]{2,1,0:T(8,128)(2,1)}) custom-call(bf16[128,2048]{1,0:T(8,128)(2,1)S(1)} %bitcast.43, bf16[128,2048]{1,0:T(8,128)(2,1)S(1)} %bitcast.44, bf16[128,2048]{1,0:T(8,128)(2,1)S(1)} %bitcast.45, bf16[128,2048]{1,0:T(8,128)(2,1)S(1)} %bitcast.46, ...), custom_call_target="tpu_custom_call" | custom-call | tf_op jit(solution)/shard_map/attend/pallas_call | solution.py:368
  87.7 0.5 convolution_convert_fusion.1
  88.2 57.5 %dispatch.1 = bf16[32,40,2048]{2,1,0:T(8,128)(2,1)} custom-call(bf16[8,40,2048]{2,1,0:T(8,128)(2,1)S(1)} %bitcast.42), custom_call_target="tpu_custom_call" | custom-call | tf_op jit(solution)/shard_map/dispatch/pallas_call | solution.py:392
  145.7 0.0 copy-done.6
  145.7 9.2 %fusion.12 = f32[1280,1024]{1,0:T(8,128)} fusion(bf16[1280,2048]{1,0:T(8,128)(2,1)} %bitcast.48, bf16[1,2048,1024]{2,1,0:T(8,128)(2,1)S(1)} %copy-done.6), kind=kOutput, calls=%fused_computation.14 | convolution fusion | flops 5368709120 | bytes 14680064 | tf_op jit(solution)/shard_map/dot_general | solution.py:407
  154.9 20.0 %convert_bitcast_fusion.1 = bf16[1,2048,1024]{2,1,0:T(8,128)(2,1)} fusion(bf16[1280,2048]{1,0:T(8,128)(2,1)} %bitcast.49, f32[1280,1024]{1,0:T(8,128)} %fusion.12, bf16[1280,2048]{1,0:T(8,128)(2,1)} %bitcast.53, bf16[1,1024,2048]{2,1,0:T(8,128)(2,1)} %param.17), kind=kOutput, calls=%fused_computation.17 | convolution fusion | flops 10765729792 | bytes 24117248 | tf_op jit(solution)/shard_map/dot_general | solution.py:414
  174.9 0.0 copy-start.7
  175.0 0.0 copy-start.8
  175.0 11.3 %convert_bitcast_fusion = bf16[1,1024,2048]{2,1,0:T(8,128)(2,1)} fusion(bf16[1280,2048]{1,0:T(8,128)(2,1)} %bitcast.54, f32[1280,1024]{1,0:T(8,128)} %fusion.12), kind=kOutput, calls=%fused_computation.16 | convolution fusion | flops 5382602752 | bytes 14680064 | tf_op jit(solution)/shard_map/dot_general | solution.py:417
  186.3 0.0 copy-done.7
  186.3 0.0 copy-done.8
  186.3 7.8 %convolution_convert_fusion = bf16[1280,2048]{1,0:T(8,128)(2,1)} fusion(bf16[1,1024,2048]{2,1,0:T(8,128)(2,1)S(1)} %copy-done.7, f32[1280,1024]{1,0:T(8,128)S(1)} %copy-done.8), kind=kOutput, calls=%fused_computation | convolution fusion | flops 5383127040 | bytes 14680064 | tf_op jit(solution)/shard_map/dot_general | solution.py:420
  194.1 69.8 %combine.1 = bf16[8,40,2048]{2,1,0:T(8,128)(2,1)S(1)} custom-call(bf16[32,40,2048]{2,1,0:T(8,128)(2,1)} %bitcast.50), custom_call_target="tpu_custom_call" | custom-call | tf_op jit(solution)/shard_map/combine/pallas_call | solution.py:422
  263.9 1.3 fusion.15
Async XLA Ops:
  0.6 2.5 copy-start
  3.6 1.0 copy-start.1
  4.7 1.0 copy-start.2
  5.7 1.0 copy-start.3
  6.7 1.0 copy-start.4
  7.8 0.7 copy-start.5
  8.5 137.3 %copy-start.6 = (bf16[1,2048,1024]{2,1,0:T(8,128)(2,1)S(1)}, bf16[1,2048,1024]{2,1,0:T(8,128)(2,1)}, u32[]{:S(2)}) copy-start(bf16[1,2048,1024]{2,1,0:T(8,128)(2,1)} %param.16) | copy-start | bytes 12582916
  174.9 11.3 %copy-start.7 = (bf16[1,1024,2048]{2,1,0:T(8,128)(2,1)S(1)}, bf16[1,1024,2048]{2,1,0:T(8,128)(2,1)}, u32[]{:S(2)}) copy-start(bf16[1,1024,2048]{2,1,0:T(8,128)(2,1)} %param.17) | copy-start | bytes 12582916
  175.0 11.3 %copy-start.8 = (f32[1280,1024]{1,0:T(8,128)S(1)}, f32[1280,1024]{1,0:T(8,128)}, u32[]{:S(2)}) copy-start(f32[1280,1024]{1,0:T(8,128)} %fusion.12) | copy-start | bytes 15728644

commit v2 on v1

--- a/solution.py
+++ b/solution.py
@@ -61,7 +61,11 @@
         self.z_send, self.z_recv, self.f_send, self.f_recv, self.r_send, self.r_recv, self.own = sems
 
     def slot(self, group, source):
-        return self.out.at[group * self.place.owners + source]
+        index = group * self.place.owners + source
+        if len(self.out.shape) == 3:
+            return self.out.at[index]
+        padded = self.send.shape[1]
+        return self.out.at[pl.ds(pl.multiple_of(index * padded, 8), padded)]
 
     def along(self, k):
         p = self.place
@@ -111,15 +115,29 @@
         self.forward(k, k % 2).wait_recv()
         self.relay(k).start()
 
-    def finish(self):
+    def rest_of_side(self, side):
+        for k in range(self.place.owners):
+            if k % 2 != side:
+                self.forward(k, side).wait_recv()
+
+    def corner(self):
+        for k in range(self.place.owners):
+            self.relay(k).wait_recv()
+
+    def sent(self):
         for k in range(self.place.owners):
             if k > 0:
                 self.along(k).wait_send()
             self.forward(k, 0).wait_send()
             self.forward(k, 1).wait_send()
-            self.forward(k, 1 - k % 2).wait_recv()
-            self.relay(k).wait()
+            self.relay(k).wait_send()
+
+    def finish(self):
         self.local().wait()
+        self.rest_of_side(0)
+        self.rest_of_side(1)
+        self.corner()
+        self.sent()
 
 
 def dispatch_sems(owners):
@@ -234,24 +252,98 @@
     tokens.finish()
 
 
-def dispatch_kernel(sizes, send, arrived, *sems):
+def gelu_and_slope(x):
+    root = math.sqrt(2.0 / math.pi)
+    square = x * x
+    curve = jnp.tanh(root * (x + 0.044715 * (square * x)))
+    half = 0.5 * (1.0 + curve)
+    slope = half + 0.5 * x * (1.0 - curve * curve) * (root * (1.0 + 3 * 0.044715 * square))
+    return x * half, slope
+
+
+def dispatch_kernel(sizes, send, g, w_first, w_second, arrived, hidden, d_pre,
+                    g_held, in_held, out_held, back_held, g_sem, in_sem, out_sem, *sems):
     place = Place(sizes)
+    owners = place.owners
+    loads = (
+        pltpu.make_async_copy(w_second, out_held, out_sem),
+        pltpu.make_async_copy(g, g_held, g_sem),
+        pltpu.make_async_copy(w_first, in_held, in_sem),
+    )
+    for load in loads:
+        load.start()
     place.greet()
     tokens = Dispatch(place, send, arrived, sems)
     tokens.start()
-    for n in range(place.owners):
+    pieces = 8
+    size = g_held.shape[0] // pieces
+    width = 256
+
+    def project(n):
+        back_held[n * size : (n + 1) * size, :] = lax.dot_general(
+            g_held[n * size : (n + 1) * size, :],
+            out_held[...],
+            (((1,), (1,)), ((), ())),
+            preferred_element_type=jnp.float32,
+        )
+
+    def expert(group):
+        count = owners * send.shape[1]
+        at = pl.ds(pl.multiple_of(group * count, 16), count)
+
+        @pl.loop(0, in_held.shape[1] // width)
+        def _(c):
+            cols = pl.ds(pl.multiple_of(c * width, width), width)
+            pre = jnp.dot(arrived[at, :], in_held[:, cols], preferred_element_type=jnp.float32)
+            value, slope = gelu_and_slope(pre)
+            hidden[at, cols] = value.astype(jnp.bfloat16)
+            d_pre[at, cols] = (slope * back_held[at, cols]).astype(jnp.bfloat16)
+
+    loads[0].wait()
+    loads[1].wait()
+    for n in range(owners):
+        for piece in range(n * pieces // owners, (n + 1) * pieces // owners):
+            project(piece)
         tokens.pass_on(n)
         if n > 0:
             tokens.pass_diagonal(n - 1)
-    tokens.pass_diagonal(place.owners - 1)
-    tokens.finish()
-
-
-def combine_kernel(sizes, part, returned, first, mine, onward, second, a_send, a_recv, b_send,
-                   b_recv, z_send, z_recv, own_sem):
+    tokens.pass_diagonal(owners - 1)
+    loads[2].wait()
+    tokens.local().wait()
+    expert(place.dp)
+    for side in range(2):
+        tokens.rest_of_side(side)
+        expert(place.sides[side])
+    tokens.corner()
+    expert((place.sides[0] + 2) % 4)
+    tokens.sent()
+
+
+def combine_kernel(sizes, part, x, d_pre, hidden, g, returned, grad_first, grad_second, first,
+                   mine, onward, second, x_held, d_held, h_held, g_held, a_send, a_recv, b_send,
+                   b_recv, z_send, z_recv, load_sem, own_sem):
     place = Place(sizes)
     owners = place.owners
+    loads = [
+        pltpu.make_async_copy(src, dst, load_sem.at[n])
+        for n, (src, dst) in enumerate(
+            ((x, x_held), (d_pre, d_held), (hidden, h_held), (g, g_held))
+        )
+    ]
+    for load in loads:
+        load.start()
     place.greet()
+    pieces = 8
+
+    def gradients(n):
+        for left, right, grad in ((x_held, d_held, grad_first), (h_held, g_held, grad_second)):
+            size = left.shape[1] // pieces
+            grad[n * size : (n + 1) * size, :] = lax.dot_general(
+                left[:, n * size : (n + 1) * size],
+                right[...],
+                (((0,), (0,)), ((), ())),
+                preferred_element_type=jnp.float32,
+            ).astype(jnp.bfloat16)
 
     def sides(k):
         return place.sides[k % 2], place.sides[1 - k % 2]
@@ -285,9 +377,16 @@
         )
 
     order = list(range(1, owners)) + [0]
-    for k in order:
+    ahead = min(4, owners)
+
+    def open_exchange(k):
         exchange(k, 1).start()
         exchange(k, 0).start()
+
+    for k in order[:ahead]:
+        open_exchange(k)
+    for load in loads:
+        load.wait()
 
     def add(k):
         exchange(k, 1).wait_recv()
@@ -313,7 +412,11 @@
 
     lag = 2
     for n, k in enumerate(order):
+        for done in range(n * pieces // owners, (n + 1) * pieces // owners):
+            gradients(done)
         add(k)
+        if n + ahead < owners:
+            open_exchange(order[n + ahead])
         if n >= lag:
             close(order[n - lag])
     for k in order[owners - lag :]:
@@ -329,7 +432,7 @@
 
 def params(number):
     return pltpu.CompilerParams(
-        collective_id=number, has_side_effects=True, vmem_limit_bytes=48 * 1024 * 1024
+        collective_id=number, has_side_effects=True, vmem_limit_bytes=60 * 1024 * 1024
     )
 
 
@@ -389,57 +492,66 @@
         name="attend",
     )(queries[0], keys[0], values[0], resid[0], norm_gain[None, :], placed(cotangent[0]))
 
-    arrived_x = pl.pallas_call(
-        functools.partial(dispatch_kernel, sizes),
-        out_shape=slots,
-        in_specs=[VMEM],
-        out_specs=ANY,
-        scratch_shapes=dispatch_sems(owners),
-        compiler_params=params(1),
-        name="dispatch",
-    )(placed(normed))
-
     slot_count = groups * owners * padded
-    inputs = arrived_x.reshape(slot_count, width)
     grads_in = arrived_g.reshape(slot_count, width)
     w_first = w_in[0]
     w_second = w_out[0]
-    pre_act = jnp.dot(inputs, w_first, preferred_element_type=f32)
-    activated, pull_back = jax.vjp(jax.nn.gelu, pre_act)
-    hidden = activated.astype(bf16)
-    back_proj = lax.dot_general(
-        grads_in, w_second, (((1,), (1,)), ((), ())), preferred_element_type=f32
-    )
-    d_pre = pull_back(back_proj)[0].astype(bf16)
-    grad_first = lax.dot_general(
-        inputs, d_pre, (((0,), (0,)), ((), ())), preferred_element_type=f32
-    ).astype(bf16)
-    grad_second = lax.dot_general(
-        hidden, grads_in, (((0,), (0,)), ((), ())), preferred_element_type=f32
-    ).astype(bf16)
+    units = w_first.shape[1]
+    inputs, hidden, d_pre = pl.pallas_call(
+        functools.partial(dispatch_kernel, sizes),
+        out_shape=(
+            jax.ShapeDtypeStruct((slot_count, width), bf16),
+            jax.ShapeDtypeStruct((slot_count, units), bf16),
+            jax.ShapeDtypeStruct((slot_count, units), bf16),
+        ),
+        in_specs=[VMEM, ANY, ANY, ANY],
+        out_specs=(VMEM, VMEM, VMEM),
+        scratch_shapes=[
+            pltpu.VMEM((slot_count, width), bf16),
+            pltpu.VMEM(w_first.shape, bf16),
+            pltpu.VMEM(w_second.shape, bf16),
+            pltpu.VMEM((slot_count, units), f32),
+            dma,
+            dma,
+            dma,
+            *dispatch_sems(owners),
+        ],
+        compiler_params=params(1),
+        name="dispatch",
+    )(placed(normed), grads_in, w_first, w_second)
+
     part = jnp.dot(hidden, w_second, preferred_element_type=f32).astype(bf16)
 
-    returned = pl.pallas_call(
+    returned, grad_first, grad_second = pl.pallas_call(
         functools.partial(combine_kernel, sizes),
-        out_shape=jax.ShapeDtypeStruct((owners, padded, width), bf16),
-        in_specs=[VMEM],
-        out_specs=VMEM,
+        out_shape=(
+            jax.ShapeDtypeStruct((owners, padded, width), bf16),
+            jax.ShapeDtypeStruct(w_first.shape, bf16),
+            jax.ShapeDtypeStruct(w_second.shape, bf16),
+        ),
+        in_specs=[VMEM, ANY, ANY, ANY, ANY],
+        out_specs=(VMEM, VMEM, VMEM),
         scratch_shapes=[
             pltpu.VMEM((owners, 2, padded, width), bf16),
             pltpu.VMEM((owners, padded, width), bf16),
             pltpu.VMEM((owners, padded, width), bf16),
             pltpu.VMEM((owners, padded, width), bf16),
+            pltpu.VMEM((slot_count, width), bf16),
+            pltpu.VMEM((slot_count, units), bf16),
+            pltpu.VMEM((slot_count, units), bf16),
+            pltpu.VMEM((slot_count, width), bf16),
             dma((owners, 2)),
             dma((owners, 2)),
             dma((owners,)),
             dma((owners,)),
             dma((owners,)),
             dma((owners,)),
+            dma((4,)),
             dma,
         ],
         compiler_params=params(2),
         name="combine",
-    )(part.reshape(groups * owners, padded, width))
+    )(part.reshape(groups * owners, padded, width), inputs, d_pre, hidden, grads_in)
 
     expert_rows = lax.dot_general(
         placing,

time: 266 us -> 243 us (0.914)
  matrix products: 50.6 us -> 16.6 us
  Pallas kernels: 207 us -> 216 us
    dot_general x3 -> x0, matrix products: 40.5 us -> none  [the longest x1 20 us: shards(): lax.dot_general(inputs, d_pre, (((0,), (0,)), ((), ())), preferred_elemen...]
    pallas_call x2, Pallas kernels: 127 us -> 135 us  [the longest x1 68.8 us: shards(): pl.pallas_call(functools.partial(dispatch_kernel, sizes), out_shape=(jax....]
    dot_general x2, matrix products: 0.98 us -> 4.14 us  [placed(): sent = jnp.dot(placing, x, preferred_element_type=f32).astype(bf16)]
    unnamed x18 -> x8, local copies, waits for them, and re-layouts: 4.88 us -> 6.84 us
where the time goes in v2:
time: 243 us
  Pallas kernels  216 us (89%)
  matrix products  16.6 us (7%)
  local copies, waits for them, and re-layouts  6.84 us (3%)
  other arithmetic  2.46 us (1%)
    pallas_call x1, Pallas kernels, shards(): pl.pallas_call(functools.partial(attend_kernel, sizes), out_shape=(jax.Sh...  81.8 us
    pallas_call x1, Pallas kernels, shards(): pl.pallas_call(functools.partial(dispatch_kernel, sizes), out_shape=(jax....  68.8 us
    pallas_call x1, Pallas kernels, shards(): pl.pallas_call(functools.partial(combine_kernel, sizes), out_shape=(jax.S...  65.9 us
    dot_general x1, matrix products, shards(): part = jnp.dot(hidden, w_second, preferred_element_type=f32).astype(bf16)  9.86 us
    unnamed x8, local copies, waits for them, and re-layouts  6.84 us

profile of v2, /device:TPU:25, one launch (start us, length us, event | category | flops | bytes accessed | tf_op | source)
XLA Modules:
  0.0 243.1 jit_solution(7936185710733788067)
XLA Ops:
  0.6 0.0 copy-start
  0.6 0.8 fusion.6
  1.4 0.2 reduce_window_sum.11
  1.6 0.8 select_reduce_fusion
  2.4 0.7 multiply_add_fusion
  3.1 0.0 copy-done
  3.1 1.6 convolution_convert_fusion.2
  4.7 81.8 %attend.1 = (f32[128,2048]{1,0:T(8,128)}, bf16[128,2048]{1,0:T(8,128)(2,1)}, bf16[32,40,2048]{2,1,0:T(8,128)(2,1)}) custom-call(bf16[128,2048]{1,0:T(8,128)(2,1)} %bitcast.36, bf16[128,2048]{1,0:T(8,128)(2,1)} %bitcast.37, bf16[128,2048]{1,0:T(8,128)(2,1)} %bitcast.38, bf16[128,2048]{1,0:T(8,128)(2,1)} %bitcast.39, f32[1,2048]{1,0:T(1,128)} %bitcast.40, ...), custom_call_target="tpu_custom_call" | custom-call | tf_op jit(solution)/shard_map/attend/pallas_call | solution.py:471
  86.5 2.6 %convolution_convert_fusion.1 = bf16[320,2048]{1,0:T(8,128)(2,1)} fusion(bf16[128,2048]{1,0:T(8,128)(2,1)} %get-tuple-element.13, s32[128]{0:T(128)S(1)} %multiply_add_fusion), kind=kOutput, calls=%fused_computation.1 | convolution fusion | flops 168468480 | bytes 1835520 | tf_op jit(solution)/shard_map/dot_general | solution.py:467
  89.1 68.8 %dispatch.1 = (bf16[1280,2048]{1,0:T(8,128)(2,1)}, bf16[1280,1024]{1,0:T(8,128)(2,1)}, bf16[1280,1024]{1,0:T(8,128)(2,1)}) custom-call(bf16[8,40,2048]{2,1,0:T(8,128)(2,1)} %bitcast.28, bf16[1280,2048]{1,0:T(8,128)(2,1)} %bitcast.26, bf16[2048,1024]{1,0:T(8,128)(2,1)} %bitcast.31, bf16[1024,2048]{1,0:T(8,128)(2,1)} %bitcast.32), custom_call_target="tpu_custom_call" | custom-call | tf_op jit(solution)/shard_map/dispatch/pallas_call | solution.py:500
  157.9 9.9 %convolution_convert_fusion = bf16[1280,2048]{1,0:T(8,128)(2,1)} fusion(bf16[1280,1024]{1,0:T(8,128)(2,1)} %get-tuple-element.15.hidden, bf16[1,1024,2048]{2,1,0:T(8,128)(2,1)} %param.17), kind=kOutput, calls=%fused_computation | convolution fusion | flops 5371330560 | bytes 12058624 | tf_op jit(solution)/shard_map/dot_general | solution.py:523
  167.8 0.0 copy-start.2
  167.8 65.9 %combine.1 = (bf16[8,40,2048]{2,1,0:T(8,128)(2,1)}, bf16[2048,1024]{1,0:T(8,128)(2,1)}, bf16[1024,2048]{1,0:T(8,128)(2,1)}) custom-call(bf16[32,40,2048]{2,1,0:T(8,128)(2,1)} %bitcast.29, bf16[1280,2048]{1,0:T(8,128)(2,1)} %get-tuple-element.16.x, bf16[1280,1024]{1,0:T(8,128)(2,1)} %get-tuple-element.17.d_pre, bf16[1280,1024]{1,0:T(8,128)(2,1)} %get-tuple-element.15.hidden, ...), custom_call_target="tpu_custom_call" | custom-call | tf_op jit(solution)/shard_map/combine/pallas_call | solution.py:525
  233.6 0.0 copy-done.2
  233.6 2.6 %fusion.1 = bf16[1,128,2048]{2,1,0:T(8,128)(2,1)} fusion(f32[128,2048]{1,0:T(8,128)S(1)} %copy-done.2, bf16[320,2048]{1,0:T(8,128)(2,1)} %bitcast.35, s32[128]{0:T(128)S(1)} %multiply_add_fusion), kind=kOutput, calls=%fused_computation.5 | convolution fusion | flops 168337408 | bytes 2884096 | tf_op jit(solution)/shard_map/dot_general | solution.py:556
  236.2 0.0 copy-start.1
  236.2 4.8 %copy.14 = bf16[1,2048,1024]{2,1,0:T(8,128)(2,1)} copy(bf16[1,2048,1024]{2,1,0:T(8,128)(2,1)} %bitcast.34) | data formatting | bytes 8388608
  241.0 0.0 copy-done.1
  241.1 2.0 copy.15
Async XLA Ops:
  0.6 2.5 %copy-start = (bf16[1,128,2048]{2,1,0:T(8,128)(2,1)S(1)}, bf16[1,128,2048]{2,1,0:T(8,128)(2,1)}, u32[]{:S(2)}) copy-start(bf16[1,128,2048]{2,1,0:T(8,128)(2,1)} %param.13) | copy-start | bytes 1572868
  167.8 65.9 %copy-start.2 = (f32[128,2048]{1,0:T(8,128)S(1)}, f32[128,2048]{1,0:T(8,128)}, u32[]{:S(2)}) copy-start(f32[128,2048]{1,0:T(8,128)} %get-tuple-element.12) | copy-start | bytes 3145732
  236.2 4.8 %copy-start.1 = (bf16[1024,2048]{1,0:T(8,128)(2,1)S(1)}, bf16[1024,2048]{1,0:T(8,128)(2,1)}, u32[]{:S(2)}) copy-start(bf16[1024,2048]{1,0:T(8,128)(2,1)} %get-tuple-element.20) | copy-start | bytes 12582916
